TPU v7x, 32 devices: a whole 2x2x4 slice. The times are simulated.
32 devices in a mesh: row: 4 (over y, x), col: 8 (over z, core).
Axes of the slice: x: 2, y: 2, z: 4, core: 2. Of those that a mesh axis runs over, the one named last changes fastest.
Arguments:
- vectors: bfloat16 [64, 131072], P(None, ('col', 'row')), may hold values from -6 to 6
- blocks: bfloat16 [4, 4096, 128, 128], P('row', 'col'), may hold values from -0.1875 to 0.1875
- block_rows: int32 [4, 4096], P('row', 'col'), may hold values from 0 to 255, as said below
- block_cols: int32 [4, 4096], P('row', 'col'), may hold values from 0 to 127, as said below
- counts: int32 [4, 8], P('row', 'col'), may hold values from 1 to 512, as said below
Outputs:
- result: float32 [64, 131072], P(None, ('row', 'col'))
Inputs may be any that keep to these rules, and one draw needn't show every extreme that they name: Within one owner pair the slots below its count name distinct positions (block_rows, block_cols) of its 256 x 256/2 grid of blocks; later slots hold 0. `block_cols`: see block_rows. `counts`: some owner pair holds exactly 512 blocks, and some other exactly one.
All inputs are finite; a program needn't handle non-finite values.
Results may differ from a plain program's by a relative error of at most 0.0029.
Values may be sent and summed in bfloat16 or wider, within the bound.
No kernel may reach another device: no remote copies, remote signals or barrier semaphores. Data moves between devices by JAX's collectives and lax.ppermute only.
A program may use at most 128 MiB of HBM per device.

v0:
```python
import jax
import jax.numpy as jnp
from jax import lax
from jax.sharding import PartitionSpec as P


def from_root(block, axis, owner):
    block = jnp.where(lax.axis_index(axis) == owner, block, jnp.zeros_like(block))
    return lax.psum(block, axis)


def block_product(vec_panel, blocks, block_rows, block_cols, counts):
    slot_total = blocks.shape[1]
    tile_size = blocks.shape[2]
    vec_width = vec_panel.shape[0]
    row_blocks = 2 * vec_panel.shape[1] // tile_size
    vec_tiles = vec_panel.reshape(vec_width, -1, tile_size)
    picked = jnp.take(vec_tiles, block_cols.reshape(-1), axis=1)
    product = jnp.einsum("ksc,src->ksr", picked, blocks[0], preferred_element_type=jnp.float32)
    live_slots = jnp.arange(slot_total, dtype=jnp.int32) < counts.reshape(())
    owner_map = (block_rows == jnp.arange(row_blocks, dtype=jnp.int32)[:, None]) & live_slots[
        None, :
    ]
    summed = jnp.einsum(
        "is,ksr->kir", owner_map.astype(jnp.float32), product, precision=lax.Precision.HIGHEST
    )
    return summed.reshape(vec_width, row_blocks * tile_size)


def relay_group(group_rows):
    half_width = group_rows.shape[1] // 2
    col_owner = lax.axis_index("col")
    own_half = lax.dynamic_slice_in_dim(group_rows, col_owner % 2 * half_width, half_width, 1)
    return from_root(own_half, "row", col_owner // 2)


def shards(vectors, blocks, block_rows, block_cols, counts):
    vec_panel = lax.all_gather(vectors, "row", axis=1, tiled=True)
    first_part = block_product(vec_panel, blocks, block_rows, block_cols, counts)
    group_rows = lax.psum(first_part, "col").astype(jnp.bfloat16)
    second_panel = relay_group(group_rows)
    second_part = block_product(second_panel, blocks, block_rows, block_cols, counts)
    return lax.psum_scatter(second_part, "col", scatter_dimension=1, tiled=True)


def solution(mesh):
    in_specs = (
        P(None, ("col", "row")),
        P("row", "col", None, None),
        P("row", "col"),
        P("row", "col"),
        P("row", "col"),
    )
    out_specs = P(None, ("row", "col"))
    return jax.shard_map(shards, mesh=mesh, in_specs=in_specs, out_specs=out_specs, check_vma=False)
```

profile of v0, /device:TPU:0, one launch (start us, length us, event | category | flops | bytes accessed | tf_op | source)
XLA Modules:
  0.0 559.0 jit_solution(10236251056222093758)
XLA Ops:
  6.5 0.0 all-gather.2.cloned.1.call-start
  6.5 0.7 all-gather.2.cloned.1.call-update
  7.3 0.0 all-reduce.3.cloned.1.call-start
  8.0 0.7 compare_select_fusion
  8.7 0.7 compare_and_fusion
  9.4 37.7 %all-gather.2.cloned.1.call-done = bf16[64,16384]{1,0:T(8,128)(2,1)} async-done(((bf16[64,4096]{1,0:T(8,128)(2,1)}), bf16[64,16384]{1,0:T(8,128)(2,1)}) %all-gather.2.cloned.1.call-update) | async-done | bytes 2097168 | tf_op jit(solution)/shard_map/all_gather | solution.py:38
  47.1 2.2 copy_bitcast_fusion.3
  49.3 13.5 %gather_fusion = bf16[512,64,128]{2,1,0:T(8,128)(2,1)} fusion(bf16[64,128,128]{2,0,1:T(8,128)(2,1)S(1)} %copy_bitcast_fusion.3, s32[1024]{0:T(1024)S(1)} %pad_clamp_fusion), kind=kCustom, calls=%fused_computation.clone | custom fusion | bytes 16779264 | tf_op jit(solution)/shard_map/jit(_take)/gather | solution.py:18
  62.8 0.0 copy-start
  62.8 20.4 %fusion.8 = f32[64,512,128]{2,0,1:T(8,128)} fusion(bf16[1,512,128,128]{3,2,1,0:T(8,128)(2,1)} %param.8, bf16[512,64,128]{2,1,0:T(8,128)(2,1)} %gather_fusion, pred[512]{0:T(512)(128)(4,1)S(1)} %compare_and_fusion), kind=kOutput, calls=%fused_computation.10 | convolution fusion | flops 1077936128 | bytes 41943552 | tf_op jit(solution)/shard_map/ksc,src->ksr/dot_general | solution.py:19
  83.2 0.0 copy-done
  83.2 27.8 %fusion.22 = f32[64,256,128]{1,2,0:T(8,128)} fusion(f32[64,512,128]{2,0,1:T(8,128)} %fusion.8, s32[512]{0:T(512)S(1)} %bitcast.53, pred[512]{0:T(512)(128)(4,1)S(1)} %iota_compare_fusion.1), kind=kOutput, calls=%fused_computation.23 | convolution fusion | flops 12885164032 | bytes 25168384 | tf_op jit(solution)/shard_map/is,ksr->kir/dot_general | solution.py:24
  111.0 9.2 %copy.10 = f32[64,256,128]{2,1,0:T(8,128)} copy(f32[64,256,128]{1,2,0:T(8,128)} %fusion.22) | data formatting | bytes 16777216 | tf_op jit(solution)/shard_map/is,ksr->kir/transpose | solution.py:24
  120.2 11.3 %copy.31 = f32[8,8,256,128]{3,1,2,0:T(8,128)} copy(f32[8,8,256,128]{3,2,1,0:T(8,128)} %bitcast.50) | data formatting | bytes 16777216
  131.5 170.1 %all-reduce.4 = bf16[64,32768]{1,0:T(8,128)(2,1)} all-reduce(f32[64,32768]{1,0:T(8,128)} %bitcast.51), channel_id=1, replica_groups=mesh['row'=4,'col'=8] {'col'}, use_global_device_ids=true, to_apply=%region_0.0 | all-reduce | flops 2097152 | bytes 12582912 | tf_op jit(solution)/shard_map/psum | solution.py:40
  301.6 3.5 copy_bitcast_fusion.2
  305.1 0.0 all-reduce.3.cloned.1.call-update
  305.1 0.0 reduce-scatter.2.cloned.1.call-start
  305.2 67.0 %all-reduce.3.cloned.1.call-done = bf16[64,128,128]{2,0,1:T(8,128)(2,1)} async-done(((bf16[64,128,128]{2,0,1:T(8,128)(2,1)}), bf16[64,128,128]{2,0,1:T(8,128)(2,1)}) %all-reduce.3.cloned.1.call-update) | async-done | bytes 2097168 | tf_op jit(solution)/shard_map/psum | solution.py:9
  372.2 21.6 %gather_fusion.1 = bf16[512,64,128]{2,1,0:T(8,128)(2,1)} fusion(bf16[64,128,128]{2,0,1:T(8,128)(2,1)} %all-reduce.3.cloned.1.call-done, s32[1024]{0:T(1024)S(1)} %pad_clamp_fusion), kind=kCustom, calls=%fused_computation.1.clone | custom fusion | bytes 16779264 | tf_op jit(solution)/shard_map/jit(_take)/gather | solution.py:18
  393.8 20.5 %fusion.11 = f32[64,512,128]{2,0,1:T(8,128)} fusion(bf16[1,512,128,128]{3,2,1,0:T(8,128)(2,1)} %param.8, bf16[512,64,128]{2,1,0:T(8,128)(2,1)} %gather_fusion.1, pred[512]{0:T(512)(128)(4,1)S(1)} %compare_and_fusion), kind=kOutput, calls=%fused_computation.11 | convolution fusion | flops 1077936128 | bytes 41943552 | tf_op jit(solution)/shard_map/ksc,src->ksr/dot_general | solution.py:19
  414.3 27.8 %fusion.25 = f32[64,256,128]{1,2,0:T(8,128)} fusion(f32[64,512,128]{2,0,1:T(8,128)} %fusion.11, s32[512]{0:T(512)S(1)} %bitcast.54, pred[512]{0:T(512)(128)(4,1)S(1)} %iota_compare_fusion.1), kind=kOutput, calls=%fused_computation.24 | convolution fusion | flops 12885164032 | bytes 25168384 | tf_op jit(solution)/shard_map/is,ksr->kir/dot_general | solution.py:24
  442.0 9.2 %copy.13 = f32[64,256,128]{2,1,0:T(8,128)} copy(f32[64,256,128]{1,2,0:T(8,128)} %fusion.25) | data formatting | bytes 16777216 | tf_op jit(solution)/shard_map/is,ksr->kir/transpose | solution.py:24
  451.2 11.3 %copy.30 = f32[8,8,256,128]{3,1,2,0:T(8,128)} copy(f32[8,8,256,128]{3,2,1,0:T(8,128)} %bitcast.52) | data formatting | bytes 16777216
  462.5 0.0 reduce-scatter.2.cloned.1.call-update
  462.6 89.7 %reduce-scatter.2.cloned.1.call-done = f32[64,4096]{1,0:T(8,128)} async-done(((f32[64,32768]{1,0:T(8,128)}), f32[64,4096]{1,0:T(8,128)}) %reduce-scatter.2.cloned.1.call-update) | async-done | bytes 1048592 | tf_op jit(solution)/shard_map/reduce_scatter | solution.py:43
  (2 shorter events, 0.0 us)
Async XLA Ops:
  6.5 40.6 %all-gather.2.cloned.1.call-start = ((), (), s32[]{:S(2)}) async-start(), calls=%async_computation.1 | async-start | bytes 2621440 | tf_op jit(solution)/shard_map/all_gather | solution.py:38
  7.3 364.9 %all-reduce.3.cloned.1.call-start = ((), (), s32[]{:S(2)}) async-start(), calls=%async_computation.2 | async-start | bytes 4194304 | tf_op jit(solution)/shard_map/psum | solution.py:9
  62.8 20.5 %copy-start = (s32[1,512]{1,0:T(1,128)S(1)}, s32[1,512]{1,0:T(1,128)}, u32[]{:S(2)}) copy-start(s32[1,512]{1,0:T(1,128)} %param.9) | copy-start | bytes 6148
  305.1 247.1 %reduce-scatter.2.cloned.1.call-start = ((), (), s32[]{:S(2)}) async-start(), calls=%async_computation.3 | async-start | bytes 9437184 | tf_op jit(solution)/shard_map/reduce_scatter | solution.py:43
Sparse Core Ops, SparseCore 0:
  9.2 37.8 all-gather.1
  305.3 66.8 all-reduce.2
  462.7 89.5 reduce-scatter.1
where the time goes:
time: 565 us; the launch traced here: 559 us
  waiting for transfers between devices  195 us (35%)
  blocking collectives  170 us (30%)
  matrix products  96.5 us (17%)
  local copies, waits for them, and re-layouts  78.3 us (14%)
  between operations  14 us (2%)
    psum x1, blocking collectives, shards(): group_rows = lax.psum(first_part, 'col').astype(jnp.bfloat16)  170 us
    reduce_scatter x1, waiting for transfers between devices, shards(): return lax.psum_scatter(second_part, 'col', scatter_dimension=1, tiled=True)  89.7 us
    psum x1, waiting for transfers between devices, from_root(): return lax.psum(block, axis)  67 us
    dot_general x2, matrix products, block_product(): jnp.einsum('is,ksr->kir', owner_map.astype(jnp.float32), product, precisi...  55.6 us
    dot_general x2, matrix products, block_product(): jnp.einsum('ksc,src->ksr', picked, blocks[0], preferred_element_type=jnp....  40.9 us
    all_gather x1, waiting for transfers between devices, shards(): vec_panel = lax.all_gather(vectors, 'row', axis=1, tiled=True)  37.7 us
    gather x2, local copies, waits for them, and re-layouts, block_product(): picked = jnp.take(vec_tiles, block_cols.reshape(-1), axis=1)  35.1 us
    unnamed x4, local copies, waits for them, and re-layouts  22.7 us
  transfers between devices with their start and end apart: 3, of which 3 were waited for; matrix products, arithmetic and copies ran while one was open for 0% of the time, Pallas kernels for 0%

commit v1 on v0

--- a/solution.py
+++ b/solution.py
@@ -2,6 +2,18 @@
 import jax.numpy as jnp
 from jax import lax
 from jax.sharding import PartitionSpec as P
+
+
+def collect(shard, axis, dim):
+    ways, here, turn = (lax.axis_size(axis), lax.axis_index(axis), shard.shape[dim])
+    line, have = (shard, 1)
+    while have < ways:
+        line = jnp.concatenate(
+            [line, lax.ppermute(line, axis, [(d, (d - have) % ways) for d in range(ways)])],
+            axis=dim,
+        )
+        have = 2 * have
+    return jnp.roll(line, here * turn, axis=dim)
 
 
 def from_root(block, axis, owner):
@@ -35,7 +47,7 @@
 
 
 def shards(vectors, blocks, block_rows, block_cols, counts):
-    vec_panel = lax.all_gather(vectors, "row", axis=1, tiled=True)
+    vec_panel = collect(vectors, "row", 1)
     first_part = block_product(vec_panel, blocks, block_rows, block_cols, counts)
     group_rows = lax.psum(first_part, "col").astype(jnp.bfloat16)
     second_panel = relay_group(group_rows)

time: 565 us -> 568 us (level)
    all_gather x1 -> x0, waiting for transfers between devices: 37.7 us -> none  [shards(): vec_panel = lax.all_gather(vectors, 'row', axis=1, tiled=True)]
    ppermute x0 -> x2, waiting for transfers between devices: none -> 30.9 us  [collect(): lax.ppermute(line, axis, [(d, (d - have) % ways) for d in range(ways)])]
    unnamed x4 -> x9, local copies, waits for them, and re-layouts: 22.7 us -> 24.9 us
  transfers between devices with their start and end apart: 3 -> 4, of which waited for: 3 -> 4; matrix products, arithmetic and copies ran while one was open for 0% -> 0% of each run, Pallas kernels for 0% -> 0%
where the time goes in v1:
time: 568 us; the launch traced here: 561 us
  waiting for transfers between devices  191 us (34%)
  blocking collectives  169 us (30%)
  matrix products  96.5 us (17%)
  local copies, waits for them, and re-layouts  79.1 us (14%)
  between operations  14.4 us (3%)
  other arithmetic  6.01 us (1%)
    psum x1, blocking collectives, shards(): group_rows = lax.psum(first_part, 'col').astype(jnp.bfloat16)  169 us
    reduce_scatter x1, waiting for transfers between devices, shards(): return lax.psum_scatter(second_part, 'col', scatter_dimension=1, tiled=True)  89.7 us
    psum x1, waiting for transfers between devices, from_root(): return lax.psum(block, axis)  70 us
    dot_general x2, matrix products, block_product(): jnp.einsum('is,ksr->kir', owner_map.astype(jnp.float32), product, precisi...  55.6 us
    dot_general x2, matrix products, block_product(): jnp.einsum('ksc,src->ksr', picked, blocks[0], preferred_element_type=jnp....  40.9 us
    gather x2, local copies, waits for them, and re-layouts, block_product(): picked = jnp.take(vec_tiles, block_cols.reshape(-1), axis=1)  35.1 us
    ppermute x2, waiting for transfers between devices, collect(): lax.ppermute(line, axis, [(d, (d - have) % ways) for d in range(ways)])  30.9 us
    unnamed x9, local copies, waits for them, and re-layouts  24.9 us
  transfers between devices with their start and end apart: 4, of which 4 were waited for; matrix products, arithmetic and copies ran while one was open for 0% of the time, Pallas kernels for 0%

profile of v1, /device:TPU:0, one launch (start us, length us, event | category | flops | bytes accessed | tf_op | source)
XLA Modules:
  0.0 560.8 jit_solution(15833295295872210940)
XLA Ops:
  6.5 0.0 all-reduce.3.cloned.1.call-start
  6.5 3.9 collective-permute-start
  11.1 0.7 compare_and_fusion
  11.8 0.7 compare_select_fusion
  12.5 9.5 %collective-permute-done = bf16[64,4096]{1,0:T(8,128)(2,1)S(1)} collective-permute-done((bf16[64,4096]{1,0:T(8,128)(2,1)}, bf16[64,4096]{1,0:T(8,128)(2,1)S(1)}, u32[]{:S(2)}, u32[]{:S(2)}) %collective-permute-start) | collective-permute-done | bytes 524320 | tf_op jit(solution)/shard_map/ppermute | solution.py:12
  22.0 1.1 pad_maximum_fusion
  23.1 1.5 collective-permute-start.1
  24.6 1.1 constant_dynamic-update-slice_fusion.5
  25.7 21.5 %collective-permute-done.1 = bf16[64,8192]{1,0:T(8,128)(2,1)S(1)} collective-permute-done((bf16[64,8192]{1,0:T(8,128)(2,1)S(1)}, bf16[64,8192]{1,0:T(8,128)(2,1)S(1)}, u32[]{:S(2)}, u32[]{:S(2)}) %collective-permute-start.1) | collective-permute-done | bytes 1048608 | tf_op jit(solution)/shard_map/ppermute | solution.py:12
  47.2 0.1 constant_dynamic-update-slice_fusion.3
  47.3 1.1 constant_dynamic-update-slice_fusion.2
  48.4 0.1 constant_dynamic-update-slice_fusion
  48.5 0.6 copy_bitcast_fusion.3
  49.1 13.5 %gather_fusion = bf16[512,64,128]{2,1,0:T(8,128)(2,1)} fusion(bf16[64,128,128]{2,0,1:T(8,128)(2,1)S(1)} %copy_bitcast_fusion.3, s32[1024]{0:T(1024)S(1)} %pad_clamp_fusion), kind=kCustom, calls=%fused_computation.clone | custom fusion | bytes 16779264 | tf_op jit(solution)/shard_map/jit(_take)/gather | solution.py:30
  62.5 0.0 copy-start
  62.5 20.4 %fusion.8 = f32[64,512,128]{2,0,1:T(8,128)} fusion(bf16[1,512,128,128]{3,2,1,0:T(8,128)(2,1)} %param.8, bf16[512,64,128]{2,1,0:T(8,128)(2,1)} %gather_fusion, pred[512]{0:T(512)(128)(4,1)S(1)} %compare_and_fusion), kind=kOutput, calls=%fused_computation.10 | convolution fusion | flops 1077936128 | bytes 41943552 | tf_op jit(solution)/shard_map/ksc,src->ksr/dot_general | solution.py:31
  83.0 0.0 copy-done
  83.0 27.8 %fusion.22 = f32[64,256,128]{1,2,0:T(8,128)} fusion(f32[64,512,128]{2,0,1:T(8,128)} %fusion.8, s32[512]{0:T(512)S(1)} %bitcast.53, pred[512]{0:T(512)(128)(4,1)S(1)} %iota_compare_fusion.1), kind=kOutput, calls=%fused_computation.23 | convolution fusion | flops 12885164032 | bytes 25168384 | tf_op jit(solution)/shard_map/is,ksr->kir/dot_general | solution.py:36
  110.8 9.2 %copy.10 = f32[64,256,128]{2,1,0:T(8,128)} copy(f32[64,256,128]{1,2,0:T(8,128)} %fusion.22) | data formatting | bytes 16777216 | tf_op jit(solution)/shard_map/is,ksr->kir/transpose | solution.py:36
  120.0 11.3 %copy.31 = f32[8,8,256,128]{3,1,2,0:T(8,128)} copy(f32[8,8,256,128]{3,2,1,0:T(8,128)} %bitcast.50) | data formatting | bytes 16777216
  131.3 168.8 %all-reduce.4 = bf16[64,32768]{1,0:T(8,128)(2,1)} all-reduce(f32[64,32768]{1,0:T(8,128)} %bitcast.51), channel_id=1, replica_groups=mesh['row'=4,'col'=8] {'col'}, use_global_device_ids=true, to_apply=%region_0.2 | all-reduce | flops 2097152 | bytes 12582912 | tf_op jit(solution)/shard_map/psum | solution.py:52
  300.1 3.5 copy_bitcast_fusion.2
  303.6 0.0 all-reduce.3.cloned.1.call-update
  303.6 0.0 reduce-scatter.2.cloned.1.call-start
  303.7 70.0 %all-reduce.3.cloned.1.call-done = bf16[64,128,128]{2,0,1:T(8,128)(2,1)} async-done(((bf16[64,128,128]{2,0,1:T(8,128)(2,1)}), bf16[64,128,128]{2,0,1:T(8,128)(2,1)}) %all-reduce.3.cloned.1.call-update) | async-done | bytes 2097168 | tf_op jit(solution)/shard_map/psum | solution.py:21
  373.6 21.6 %gather_fusion.1 = bf16[512,64,128]{2,1,0:T(8,128)(2,1)} fusion(bf16[64,128,128]{2,0,1:T(8,128)(2,1)} %all-reduce.3.cloned.1.call-done, s32[1024]{0:T(1024)S(1)} %pad_clamp_fusion), kind=kCustom, calls=%fused_computation.1.clone | custom fusion | bytes 16779264 | tf_op jit(solution)/shard_map/jit(_take)/gather | solution.py:30
  395.3 20.5 %fusion.11 = f32[64,512,128]{2,0,1:T(8,128)} fusion(bf16[1,512,128,128]{3,2,1,0:T(8,128)(2,1)} %param.8, bf16[512,64,128]{2,1,0:T(8,128)(2,1)} %gather_fusion.1, pred[512]{0:T(512)(128)(4,1)S(1)} %compare_and_fusion), kind=kOutput, calls=%fused_computation.11 | convolution fusion | flops 1077936128 | bytes 41943552 | tf_op jit(solution)/shard_map/ksc,src->ksr/dot_general | solution.py:31
  415.7 27.8 %fusion.25 = f32[64,256,128]{1,2,0:T(8,128)} fusion(f32[64,512,128]{2,0,1:T(8,128)} %fusion.11, s32[512]{0:T(512)S(1)} %bitcast.54, pred[512]{0:T(512)(128)(4,1)S(1)} %iota_compare_fusion.1), kind=kOutput, calls=%fused_computation.24 | convolution fusion | flops 12885164032 | bytes 25168384 | tf_op jit(solution)/shard_map/is,ksr->kir/dot_general | solution.py:36
  443.5 9.2 %copy.13 = f32[64,256,128]{2,1,0:T(8,128)} copy(f32[64,256,128]{1,2,0:T(8,128)} %fusion.25) | data formatting | bytes 16777216 | tf_op jit(solution)/shard_map/is,ksr->kir/transpose | solution.py:36
  452.7 11.3 %copy.30 = f32[8,8,256,128]{3,1,2,0:T(8,128)} copy(f32[8,8,256,128]{3,2,1,0:T(8,128)} %bitcast.52) | data formatting | bytes 16777216
  464.0 0.0 reduce-scatter.2.cloned.1.call-update
  464.0 89.7 %reduce-scatter.2.cloned.1.call-done = f32[64,4096]{1,0:T(8,128)} async-done(((f32[64,32768]{1,0:T(8,128)}), f32[64,4096]{1,0:T(8,128)}) %reduce-scatter.2.cloned.1.call-update) | async-done | bytes 1048592 | tf_op jit(solution)/shard_map/reduce_scatter | solution.py:55
  (4 shorter events, 0.1 us)
Async XLA Ops:
  6.5 367.1 %all-reduce.3.cloned.1.call-start = ((), (), s32[]{:S(2)}) async-start(), calls=%async_computation.1 | async-start | bytes 4194304 | tf_op jit(solution)/shard_map/psum | solution.py:21
  6.5 15.4 %collective-permute-start = (bf16[64,4096]{1,0:T(8,128)(2,1)}, bf16[64,4096]{1,0:T(8,128)(2,1)S(1)}, u32[]{:S(2)}, u32[]{:S(2)}) collective-permute-start(bf16[64,4096]{1,0:T(8,128)(2,1)} %param.7), channel_id=1, source_target_pairs={{0,24},{8,0},{16,8},{24,16},{1,25},{9,1},{17,9},{25,17},{2,26},{10... | collective-permute-start | bytes 1572872 | tf_op jit(solution)/shard_map/ppermute | solution.py:12
  23.1 24.1 %collective-permute-start.1 = (bf16[64,8192]{1,0:T(8,128)(2,1)S(1)}, bf16[64,8192]{1,0:T(8,128)(2,1)S(1)}, u32[]{:S(2)}, u32[]{:S(2)}) collective-permute-start(bf16[64,8192]{1,0:T(8,128)(2,1)S(1)} %pad_maximum_fusion), channel_id=1, source_target_pairs={{0,16},{8,24},{16,0},{24,8},{1,17},{9,25},{17,1},{25,9},{2,18},{10... | collective-permute-start | bytes 3145736 | tf_op jit(solution)/shard_map/ppermute | solution.py:12
  62.5 20.4 %copy-start = (s32[1,512]{1,0:T(1,128)S(1)}, s32[1,512]{1,0:T(1,128)}, u32[]{:S(2)}) copy-start(s32[1,512]{1,0:T(1,128)} %param.9) | copy-start | bytes 6148
  303.6 250.1 %reduce-scatter.2.cloned.1.call-start = ((), (), s32[]{:S(2)}) async-start(), calls=%async_computation.2 | async-start | bytes 9437184 | tf_op jit(solution)/shard_map/reduce_scatter | solution.py:55
Sparse Core Ops, SparseCore 0:
  303.7 69.8 all-reduce.2
  464.2 89.5 reduce-scatter.1
